TPU v7x, 32 devices: a whole 2x2x4 slice. The times are simulated.
32 devices in a mesh: rows: 8 (over z, x), wide: 4 (over y, core).
Axes of the slice: x: 2, y: 2, z: 4, core: 2. Of those that a mesh axis runs over, the one named last changes fastest.
Arguments:
- hidden_in: bfloat16 [1024, 16, 1024], P('wide', 'rows'), may hold values from -6 to 6
- segments: int32 [16, 1024], P('rows'), may hold values from 0 to 3, never falling along the last dimension, each value on 1 to 768 neighbouring positions
- prefix_vis: int32 [16, 64], P('rows'), may hold values 0 or 1
- prefix_key: bfloat16 [64, 1024], replicated, may hold values from -6 to 6
- prefix_value: bfloat16 [64, 1024], replicated, may hold values from -6 to 6
- w_query: bfloat16 [1024, 1024], replicated, may hold values from -0.375 to 0.375
- w_key: bfloat16 [1024, 1024], replicated, may hold values from -0.1875 to 0.1875
- w_value: bfloat16 [1024, 1024], replicated, may hold values from -0.1875 to 0.1875
- w_out: bfloat16 [1024, 1024], replicated, may hold values from -4 to 4
- norm1_gain: float32 [1024], replicated, may hold values from 0.1 to 1.9
- norm1_bias: float32 [1024], replicated, may hold values from -3 to 3
- w_up: bfloat16 [1024, 4096], P(None, 'wide'), may hold values from -0.1875 to 0.1875
- w_down: bfloat16 [4096, 1024], P('wide'), may hold values from -0.09375 to 0.09375
- norm2_gain: float32 [1024], replicated, may hold values from 0.1 to 1.9
- norm2_bias: float32 [1024], replicated, may hold values from -3 to 3
- out_grad: float32 [1024, 16, 1024], P('wide', 'rows'), may hold values from -6 to 6
Outputs:
- block_out: bfloat16 [1024, 16, 1024], P('wide', 'rows')
- input_grad: float32 [1024, 16, 1024], P('wide', 'rows')
- prefix_key_grad: float32 [64, 1024], replicated
- prefix_value_grad: float32 [64, 1024], replicated
Inputs may be any that keep to these rules, and one draw needn't show every extreme that they name: `segments`: in each row the segment ids never fall, and a segment holds at most 768 positions.
All inputs are finite; a program needn't handle non-finite values. No bound on the sum of `prefix_vis` on one device may be relied on, other than what follows from the above.
Results may differ from a plain program's by a relative error of at most 0.014.
The roundings to bfloat16 on the way count: a program that leaves them out, or rounds other values in their place, can miss the bound.
Values may be sent and summed in bfloat16 or wider, within the bound.
A program may use at most 256 MiB of HBM per device.

v0:
```python
import jax
import jax.numpy as jnp
from jax import lax
from jax.sharding import PartitionSpec as P

H = 16
E = 64
P_SIZE = 64
norm_eps = 1e-05
neg_large = -1e30
root_half = 0.7071067811865476
inv_root_tau = 0.3989422804014327


def norm_forward(summed, norm_gain, norm_bias):
    average = jnp.mean(summed, axis=-1, keepdims=True)
    centred = summed - average
    variance = jnp.mean(centred * centred, axis=-1, keepdims=True)
    inv_std = lax.rsqrt(variance + norm_eps)
    scaled = centred * inv_std
    return (scaled * norm_gain + norm_bias, scaled, inv_std)


def norm_backward(grad_out, scaled, inv_std, norm_gain):
    shaped = grad_out * norm_gain
    return inv_std * (
        shaped
        - jnp.mean(shaped, axis=-1, keepdims=True)
        - scaled * jnp.mean(shaped * scaled, axis=-1, keepdims=True)
    )


def gelu_slope(hidden_pre):
    return (
        0.5 * (1.0 + lax.erf(hidden_pre * root_half))
        + hidden_pre * jnp.exp(-0.5 * hidden_pre * hidden_pre) * inv_root_tau
    )


def project(left, weight):
    return jnp.einsum("crd,de->cre", left, weight, preferred_element_type=jnp.float32)


def project_back(left, weight):
    return jnp.einsum("cre,de->crd", left, weight, preferred_element_type=jnp.float32)


def heads_of(block, model_width, first):
    picked = block[..., first * model_width : (first + 1) * model_width]
    return picked.reshape(block.shape[0], block.shape[1], H, E)


def attention_probs(query_heads, key_heads, own_seg, all_seg, prefix_vis, prefix_keys):
    seq_scores = jnp.einsum(
        "crhe,lrhe->rhcl", query_heads, key_heads, preferred_element_type=jnp.float32
    )
    pre_scores = jnp.einsum(
        "crhe,phe->rhcp", query_heads, prefix_keys, preferred_element_type=jnp.float32
    )
    same_seg = (own_seg[:, :, None] == all_seg[:, None, :])[:, None]
    visible = (prefix_vis > 0)[:, None, None, :]
    seq_scores = jnp.where(same_seg, seq_scores, neg_large)
    pre_scores = jnp.where(visible, pre_scores, neg_large)
    row_max = jnp.maximum(jnp.max(seq_scores, axis=-1), jnp.max(pre_scores, axis=-1))[..., None]
    seq_exp = jnp.exp(seq_scores - row_max)
    pre_exp = jnp.exp(pre_scores - row_max)
    prob_total = (jnp.sum(seq_exp, axis=-1) + jnp.sum(pre_exp, axis=-1))[..., None]
    seq_prob = seq_exp / prob_total
    pre_prob = pre_exp / prob_total
    return (
        seq_prob,
        pre_prob,
        seq_prob.astype(jnp.bfloat16),
        pre_prob.astype(jnp.bfloat16),
        row_max,
        prob_total,
    )


def on_device(
    hidden_in,
    segments,
    prefix_vis,
    prefix_key,
    prefix_value,
    w_query,
    w_key,
    w_value,
    w_out,
    norm1_gain,
    norm1_bias,
    w_up,
    w_down,
    norm2_gain,
    norm2_bias,
    out_grad,
):
    per_dev = hidden_in.shape[0]
    row_count = hidden_in.shape[1]
    model_width = hidden_in.shape[2]
    offset = lax.axis_index("wide") * per_dev
    own_seg = lax.dynamic_slice_in_dim(segments, offset, per_dev, 1)
    prefix_keys = prefix_key.reshape(P_SIZE, H, E)
    prefix_vals = prefix_value.reshape(P_SIZE, H, E)
    queries = (project(hidden_in, w_query) * 0.125).astype(jnp.bfloat16)
    key_own = project(hidden_in, w_key).astype(jnp.bfloat16)
    value_own = project(hidden_in, w_value).astype(jnp.bfloat16)
    pair_own = jnp.concatenate([key_own, value_own], axis=2)
    pair_all = lax.all_gather(pair_own, "wide", axis=0, tiled=True)
    query_heads = queries.reshape(per_dev, row_count, H, E)
    forward_probs = attention_probs(
        query_heads, heads_of(pair_all, model_width, 0), own_seg, segments, prefix_vis, prefix_keys
    )
    seq_prob, pre_prob, seq_low, pre_low, row_max, prob_total = forward_probs
    mixture = jnp.einsum(
        "rhcl,lrhe->crhe",
        seq_low,
        heads_of(pair_all, model_width, 1),
        preferred_element_type=jnp.float32,
    )
    mixture = mixture + jnp.einsum(
        "rhcp,phe->crhe", pre_low, prefix_vals, preferred_element_type=jnp.float32
    )
    mix_low = mixture.reshape(per_dev, row_count, model_width).astype(jnp.bfloat16)
    attn_out = project(mix_low, w_out)
    normed_one, scaled_one, inv_one = norm_forward(
        hidden_in.astype(jnp.float32) + attn_out, norm1_gain, norm1_bias
    )
    normed_low = normed_one.astype(jnp.bfloat16)

    def up_rows(row_piece):
        return jnp.einsum("lrd,df->lrf", row_piece, w_up, preferred_element_type=jnp.float32)

    hidden_pre = up_rows(lax.all_gather(normed_low, "wide", axis=0, tiled=True))
    hidden_act = jax.nn.gelu(hidden_pre, approximate=False).astype(jnp.bfloat16)
    ffn_out = lax.psum_scatter(
        jnp.einsum("lrf,fd->lrd", hidden_act, w_down, preferred_element_type=jnp.float32),
        "wide",
        scatter_dimension=0,
        tiled=True,
    )
    normed_two, scaled_two, inv_two = norm_forward(normed_one + ffn_out, norm2_gain, norm2_bias)
    block_out = normed_two.astype(jnp.bfloat16)
    grad_two = norm_backward(out_grad, scaled_two, inv_two, norm2_gain)
    grad_ffn = grad_two.astype(jnp.bfloat16)
    pre_back = up_rows(lax.all_gather(normed_low, "wide", axis=0, tiled=True))
    hidden_grad = jnp.einsum(
        "lrd,fd->lrf",
        lax.all_gather(grad_ffn, "wide", axis=0, tiled=True),
        w_down,
        preferred_element_type=jnp.float32,
    )
    pre_rows = pre_back
    grad_pre = (hidden_grad * gelu_slope(pre_rows)).astype(jnp.bfloat16)
    pre_rows = grad_pre
    ffn_back = lax.psum_scatter(
        jnp.einsum("lrf,df->lrd", pre_rows, w_up, preferred_element_type=jnp.float32),
        "wide",
        scatter_dimension=0,
        tiled=True,
    )
    grad_first = grad_two + ffn_back
    grad_sum = norm_backward(grad_first, scaled_one, inv_one, norm1_gain)
    grad_attn = grad_sum.astype(jnp.bfloat16)
    grad_mix = project_back(grad_attn, w_out).astype(jnp.bfloat16)
    grad_heads = grad_mix.reshape(per_dev, row_count, H, E)
    pair_back = lax.all_gather(pair_own, "wide", axis=0, tiled=True)
    back_probs = attention_probs(
        query_heads, heads_of(pair_back, model_width, 0), own_seg, segments, prefix_vis, prefix_keys
    )
    seq_prob, pre_prob, seq_low, pre_low, row_max, prob_total = back_probs
    key_back = heads_of(pair_back, model_width, 0)
    value_back = heads_of(pair_back, model_width, 1)
    seq_grad = jnp.einsum(
        "crhe,lrhe->rhcl", grad_heads, value_back, preferred_element_type=jnp.float32
    )
    pre_grad = jnp.einsum(
        "crhe,phe->rhcp", grad_heads, prefix_vals, preferred_element_type=jnp.float32
    )
    grad_delta = (jnp.sum(seq_prob * seq_grad, axis=-1) + jnp.sum(pre_prob * pre_grad, axis=-1))[
        ..., None
    ]
    seq_ds = (seq_prob * (seq_grad - grad_delta)).astype(jnp.bfloat16)
    pre_ds = (pre_prob * (pre_grad - grad_delta)).astype(jnp.bfloat16)
    grad_query = jnp.einsum("rhcl,lrhe->crhe", seq_ds, key_back, preferred_element_type=jnp.float32)
    grad_query = grad_query + jnp.einsum(
        "rhcp,phe->crhe", pre_ds, prefix_keys, preferred_element_type=jnp.float32
    )
    grad_query = grad_query.reshape(per_dev, row_count, model_width).astype(jnp.bfloat16)
    prefix_kpart = jnp.einsum(
        "rhcp,crhe->phe", pre_ds, query_heads, preferred_element_type=jnp.float32
    ).reshape(P_SIZE, model_width)
    prefix_vpart = jnp.einsum(
        "rhcp,crhe->phe", pre_low, grad_heads, preferred_element_type=jnp.float32
    ).reshape(P_SIZE, model_width)
    key_part = jnp.einsum(
        "rhcl,crhe->lrhe", seq_ds, query_heads, preferred_element_type=jnp.float32
    )
    value_part = jnp.einsum(
        "rhcl,crhe->lrhe", seq_low, grad_heads, preferred_element_type=jnp.float32
    )
    seq_total = key_part.shape[0]
    key_grad, value_grad = (
        lax.psum_scatter(
            key_part.reshape(seq_total, row_count, model_width).astype(jnp.bfloat16),
            "wide",
            scatter_dimension=0,
            tiled=True,
        ).astype(jnp.float32),
        lax.psum_scatter(
            value_part.reshape(seq_total, row_count, model_width).astype(jnp.bfloat16),
            "wide",
            scatter_dimension=0,
            tiled=True,
        ).astype(jnp.float32),
    )
    input_grad = grad_sum + project_back(grad_query, w_query) * 0.125
    input_grad = (
        input_grad
        + project_back(key_grad.astype(jnp.bfloat16), w_key)
        + project_back(value_grad.astype(jnp.bfloat16), w_value)
    )
    prefix_key_grad, prefix_value_grad = lax.psum((prefix_kpart, prefix_vpart), ("rows", "wide"))
    return (block_out, input_grad, prefix_key_grad, prefix_value_grad)


def solution(mesh):
    in_specs = (
        P("wide", "rows", None),
        P("rows", None),
        P("rows", None),
        P(),
        P(),
        P(),
        P(),
        P(),
        P(),
        P(),
        P(),
        P(None, "wide"),
        P("wide", None),
        P(),
        P(),
        P("wide", "rows", None),
    )
    out_specs = (P("wide", "rows", None), P("wide", "rows", None), P(), P())
    return jax.shard_map(
        on_device, mesh=mesh, in_specs=in_specs, out_specs=out_specs, check_vma=False
    )
```

profile of v0, /device:TPU:0, one launch (start us, length us, event | category | flops | bytes accessed | tf_op | source)
XLA Modules:
  0.0 737.7 jit_solution(1522463249643954753)
XLA Ops:
  7.3 3.3 fusion.75
  10.6 1.3 fusion.78
  11.9 1.5 pad_maximum_fusion
  13.5 3.9 multiply_convert_fusion.1
  17.4 1.6 copy.119
  19.2 2.0 reshape.110
  21.2 1.9 copy.128
  23.2 1.2 broadcast_compare_fusion
  24.3 1.8 bitcast_reduce_fusion
  26.1 48.4 %all-gather.4.cloned.1.call-done = bf16[1024,2,2048]{2,0,1:T(8,128)(2,1)} async-done(((bf16[256,2,2048]{2,0,1:T(8,128)(2,1)}), bf16[1024,2,2048]{2,0,1:T(8,128)(2,1)}) %all-gather.4.cloned.1.call-update) | async-done | bytes 8388624 | tf_op jit(solution)/shard_map/all_gather | solution.py:109
  74.5 5.9 fusion.148
  80.5 6.2 copy.120
  86.7 15.8 %select_reduce_fusion = (f32[2,16,256]{2,1,0:T(8,128)S(1)}, f32[2,16,256,1024]{3,2,1,0:T(8,128)}) fusion(pred[2,256,1024]{2,1,0:T(8,128)(4,1)} %broadcast_compare_fusion, bf16[256,2,16,64]{0,3,2,1:T(8,128)(2,1)S(1)} %bitcast.137, bf16[1024,2,16,64]{0,3,2,1:T(8,128)(2,1)} %bitcast.134), kind=kOutput, calls=%fused_computation.3 | convolution fusion | flops 1090510848 | bytes 39354368 | tf_op jit(solution)/shard_map/crhe,lrhe->rhcl/dot_general | solution.py:54
  102.5 14.7 %fusion.1 = f32[2,16,256]{2,1,0:T(8,128)S(1)} fusion(f32[2,16,256,1024]{3,2,1,0:T(8,128)} %get-tuple-element.35, f32[2,16,256]{2,1,0:T(8,128)S(1)} %copy_maximum_fusion, pred[2,256,1024]{2,1,0:T(8,128)(4,1)S(1)} %copy-done.14), kind=kLoop, calls=%fused_computation.5 | loop fusion | flops 25157632 | bytes 34144256 | tf_op jit(solution)/shard_map/reduce_sum | solution.py:67
  117.2 0.5 fusion.65
  117.9 0.5 fusion.142
  118.4 6.6 copy.117
  125.5 15.7 %fusion.42 = bf16[256,2,16,64]{0,3,2,1:T(8,128)(2,1)S(1)} fusion(f32[16,2,256,64]{2,3,0,1:T(8,128)S(1)} %fusion.96, bf16[1024,2,16,64]{0,3,2,1:T(8,128)(2,1)} %bitcast.141, f32[2,16,256,1024]{3,2,1,0:T(8,128)} %get-tuple-element.35, f32[2,16,256]{2,1,0:T(8,128)S(1)} %copy_add_fusion.1, f32[2,16,256]{2,1,0:T(8,128)S(1)} %copy_maximum_fusion, ...), kind=kOutput, calls=%fused_computation.62 | convolution fusion | flops 1108344832 | bytes 41484288 | tf_op jit(solution)/shard_map/rhcl,lrhe->crhe/dot_general | solution.py:115
  141.2 1.4 fusion.149
  143.0 0.9 copy-done.2
  143.9 1.4 fusion.59
  145.6 34.4 %all-gather.6.cloned.1.call-done = bf16[1024,2,1024]{2,0,1:T(8,128)(2,1)} async-done(((bf16[256,2,1024]{2,0,1:T(8,128)(2,1)}), bf16[1024,2,1024]{2,0,1:T(8,128)(2,1)}) %all-gather.6.cloned.1.call-update) | async-done | bytes 4194320 | tf_op jit(solution)/shard_map/all_gather | solution.py:134
  180.0 9.4 %fusion.57 = (u8[1024,1024]{1,0:T(8,128)(4,1)S(1)}, u8[1024,1024]{1,0:T(8,128)(4,1)S(1)}, f32[1024,2,1024]{2,0,1:T(8,128)S(1)}) fusion(bf16[1024,2,1024]{2,0,1:T(8,128)(2,1)} %all-gather.6.cloned.1.call-done, bf16[1024,1024]{1,0:T(8,128)(2,1)S(1)} %copy-done), kind=kOutput, calls=%fused_computation.92 | convolution fusion | flops 4320133120 | bytes 16777216 | tf_op jit(solution)/shard_map/lrd,df->lrf/dot_general | solution.py:132
  189.3 3.2 copy-done.56
  192.6 24.1 %fusion.21 = f32[1024,2,1024]{2,0,1:T(8,128)} fusion(f32[1024,2,1024]{2,0,1:T(8,128)S(1)} %get-tuple-element.40, bf16[1024,1024]{1,0:T(8,128)(2,1)S(1)} %copy-done.52, u8[1024,1024]{1,0:T(8,128)(4,1)S(1)} %get-tuple-element.21, u8[1024,1024]{1,0:T(8,128)(4,1)S(1)} %get-tuple-element.20), kind=kOutput, calls=%fused_computation.39 | convolution fusion | flops 4441767936 | bytes 20971520 | tf_op jit(solution)/shard_map/lrf,fd->lrd/dot_general | solution.py:137
  216.8 71.8 %reduce-scatter.5.cloned.1.call-done = f32[256,2,1024]{2,0,1:T(8,128)} async-done(((f32[1024,2,1024]{2,0,1:T(8,128)}), f32[256,2,1024]{2,0,1:T(8,128)}) %reduce-scatter.5.cloned.1.call-update) | async-done | bytes 2097168 | tf_op jit(solution)/shard_map/reduce_scatter | solution.py:136
  288.7 3.0 fusion.146
  292.0 1.2 fusion.72
  293.2 1.8 fusion.105
  295.2 34.6 %all-gather.8.cloned.1.call-done = bf16[1024,2,1024]{2,0,1:T(8,128)(2,1)} async-done(((bf16[256,2,1024]{2,0,1:T(8,128)(2,1)}), bf16[1024,2,1024]{2,0,1:T(8,128)(2,1)}) %all-gather.8.cloned.1.call-update) | async-done | bytes 4194320 | tf_op jit(solution)/shard_map/all_gather | solution.py:149
  329.7 14.6 %fusion.23 = f32[1024,2,1024]{2,0,1:T(8,128)} fusion(f32[1024,2,1024]{2,0,1:T(8,128)} %copy-done.56, bf16[1024,1024]{1,0:T(8,128)(2,1)S(1)} %copy-done, bf16[1024,2,1024]{2,0,1:T(8,128)(2,1)} %all-gather.8.cloned.1.call-done, bf16[1024,1024]{1,0:T(8,128)(2,1)} %param.28), kind=kOutput, calls=%fused_computation.40 | convolution fusion | flops 8610906112 | bytes 25165824 | tf_op jit(solution)/shard_map/lrf,df->lrd/dot_general | solution.py:157
  344.4 0.5 reduce-scatter.9.cloned.1.call-start
  344.9 71.4 %reduce-scatter.7.cloned.1.call-done = f32[256,2,1024]{2,0,1:T(8,128)} async-done(((f32[1024,2,1024]{2,0,1:T(8,128)}), f32[256,2,1024]{2,0,1:T(8,128)}) %reduce-scatter.7.cloned.1.call-update) | async-done | bytes 2097168 | tf_op jit(solution)/shard_map/reduce_scatter | solution.py:156
  416.3 4.8 fusion.145
  421.2 1.3 copy-done.16
  422.5 2.5 fusion.81
  425.0 2.3 copy.131
  427.3 26.7 %multiply_reduce_fusion = (f32[2,16,256]{2,1,0:T(8,128)S(1)}, f32[2,16,256,1024]{3,2,1,0:T(8,128)}) fusion(f32[2,16,256]{2,1,0:T(8,128)S(1)} %copy_add_fusion.1, f32[2,16,256]{2,1,0:T(8,128)S(1)} %copy_maximum_fusion, f32[2,16,256,1024]{3,2,1,0:T(8,128)} %get-tuple-element.35, pred[2,256,1024]{2,1,0:T(8,128)(4,1)S(1)} %copy-done.15, ...), kind=kOutput, calls=%fused_computation.1 | convolution fusion | flops 1115676672 | bytes 72974336 | tf_op jit(solution)/shard_map/crhe,lrhe->rhcl/dot_general | solution.py:174
  454.0 2.0 fusion.29
  456.1 28.0 %multiply_convert_fusion = bf16[2,16,256,1024]{3,2,1,0:T(8,128)(2,1)} fusion(f32[2,16,256,1024]{3,2,1,0:T(8,128)} %get-tuple-element.42, f32[2,16,256]{2,1,0:T(8,128)S(1)} %copy_add_fusion, f32[2,16,256]{2,1,0:T(8,128)S(1)} %copy_add_fusion.1, f32[2,16,256]{2,1,0:T(8,128)S(1)} %copy_maximum_fusion, f32[2,16,256,1024]{3,2,1,0:T(8,128)} %get-tuple-element.35, ...), kind=kLoop, calls=%fused_computation | loop fusion | flops 50331648 | bytes 84508672 | tf_op jit(solution)/shard_map/convert_element_type | solution.py:183
  484.1 10.8 %convolution_convert_fusion = bf16[2,16,64,1024]{3,2,1,0:T(8,128)(2,1)} fusion(bf16[256,2,16,64]{0,3,2,1:T(8,128)(2,1)S(1)} %bitcast.138, bf16[2,16,256,1024]{3,2,1,0:T(8,128)(2,1)} %multiply_convert_fusion), kind=kOutput, calls=%fused_computation.41 | convolution fusion | flops 1075838976 | bytes 22020096 | tf_op jit(solution)/shard_map/rhcl,crhe->lrhe/dot_general | solution.py:196
  494.9 6.2 copy.139
  501.4 19.3 %fusion.25 = bf16[2,16,64,1024]{3,2,1,0:T(8,128)(2,1)} fusion(bf16[256,2,16,64]{0,3,2,1:T(8,128)(2,1)} %bitcast.145, f32[2,16,256,1024]{3,2,1,0:T(8,128)} %get-tuple-element.35, f32[2,16,256]{2,1,0:T(8,128)S(1)} %copy_add_fusion.1, f32[2,16,256]{2,1,0:T(8,128)S(1)} %copy_maximum_fusion, pred[2,256,1024]{2,1,0:T(8,128)(4,1)} %broadcast_compare_fusion), kind=kOutput, calls=%fused_computation.42 | convolution fusion | flops 1109393408 | bytes 39387136 | tf_op jit(solution)/shard_map/rhcl,crhe->lrhe/dot_general | solution.py:199
  520.7 6.2 copy.140
  527.1 0.9 copy-done.21
  527.9 1.0 copy.137
  528.9 2.3 fusion.31
  531.3 0.4 fusion.91
  531.8 0.6 copy-done.12
  532.3 0.9 copy.142
  533.2 2.0 fusion.94
  535.2 0.9 copy.144
  536.0 2.0 copy.145
  538.1 13.8 %fusion.150 = f32[2,16,64,256]{3,2,1,0:T(8,128)} fusion(bf16[1024,2,16,64]{0,3,2,1:T(8,128)(2,1)} %bitcast.135, bf16[2,16,256,1024]{3,2,1,0:T(8,128)(2,1)} %multiply_convert_fusion), kind=kOutput, calls=%fused_computation.180 | convolution fusion | flops 1073741824 | bytes 23068672 | tf_op jit(solution)/shard_map/rhcl,lrhe->crhe/dot_general | solution.py:185
  551.9 2.0 fusion.28
  554.0 4.7 fusion.52
  558.7 34.4 %reduce-scatter.11.cloned.1.call-done = bf16[256,2,1024]{2,0,1:T(8,128)(2,1)} async-done(((bf16[1024,2,1024]{2,0,1:T(8,128)(2,1)}), bf16[256,2,1024]{2,0,1:T(8,128)(2,1)}) %reduce-scatter.11.cloned.1.call-update) | async-done | bytes 1048592 | tf_op jit(solution)/shard_map/reduce_scatter | solution.py:210
  593.1 2.7 fusion.48
  595.9 0.4 copy-done.24
  596.3 3.9 add_add_fusion
  600.2 2.9 copy.146
  603.1 124.2 %all-reduce.3.cloned.1.call-done = (f32[64,1024]{1,0:T(8,128)}, f32[64,1024]{1,0:T(8,128)}) async-done(((f32[64,1024]{1,0:T(8,128)}, f32[64,1024]{1,0:T(8,128)}), (f32[64,1024]{1,0:T(8,128)}, f32[64,1024]{1,0:T(8,128)})) %all-reduce.3.cloned.1.call-update) | async-done | bytes 524304 | tf_op jit(solution)/shard_map/psum | solution.py:223
  727.3 1.7 copy.203
  729.0 1.7 copy.204
  (143 shorter events, 2.5 us)
Async XLA Ops:
  7.2 172.8 %copy-start = (bf16[1024,1024]{1,0:T(8,128)(2,1)S(1)}, bf16[1024,1024]{1,0:T(8,128)(2,1)}, u32[]{:S(2)}) copy-start(bf16[1024,1024]{1,0:T(8,128)(2,1)} %param.27) | copy-start | bytes 6291460
  7.2 3.4 copy-start.27
  7.2 67.3 %all-gather.4.cloned.1.call-start = ((), (), s32[]{:S(2)}) async-start(), calls=%async_computation.4 | async-start | bytes 10485760 | tf_op jit(solution)/shard_map/all_gather | solution.py:109
  7.2 3.3 copy-start.53
  13.4 166.6 %all-gather.6.cloned.1.call-start = ((), (), s32[]{:S(2)}) async-start(), calls=%async_computation.5 | async-start | bytes 5242880 | tf_op jit(solution)/shard_map/all_gather | solution.py:134
  13.5 5.6 copy-start.36
  13.5 9.7 %copy-start.48 = (s32[2,1024]{1,0:T(2,128)S(1)}, s32[2,1024]{1,0:T(2,128)}, u32[]{:S(2)}) copy-start(s32[2,1024]{1,0:T(2,128)} %param.17) | copy-start | bytes 24580
  13.5 9.7 %copy-start.55 = (s32[2,64]{1,0:T(2,128)S(1)}, s32[2,64]{1,0:T(2,128)}, u32[]{:S(2)}) copy-start(s32[2,64]{1,0:T(2,128)} %param.18) | copy-start | bytes 1540
  19.0 67.7 %copy-start.8 = (bf16[256,2,1024]{0,2,1:T(8,128)(2,1)}, bf16[256,2,1024]{0,2,1:T(8,128)(2,1)S(1)}, u32[]{:S(2)}) copy-start(bf16[256,2,1024]{0,2,1:T(8,128)(2,1)S(1)} %copy.119) | copy-start | bytes 3145732
  19.2 61.3 %copy-start.20 = (bf16[64,16,64]{2,1,0:T(8,128)(2,1)}, bf16[64,16,64]{2,1,0:T(8,128)(2,1)S(1)}, u32[]{:S(2)}) copy-start(bf16[64,16,64]{2,1,0:T(8,128)(2,1)S(1)} %reshape.109) | copy-start | bytes 393220
  23.1 94.7 %copy-start.49 = (pred[2,64]{1,0:T(4,128)(4,1)}, pred[2,64]{1,0:T(4,128)(4,1)S(1)}, u32[]{:S(2)}) copy-start(pred[2,64]{1,0:T(4,128)(4,1)S(1)} %broadcast_compare_fusion.1) | copy-start | bytes 388
  86.7 15.8 %copy-start.14 = (pred[2,256,1024]{2,1,0:T(8,128)(4,1)S(1)}, pred[2,256,1024]{2,1,0:T(8,128)(4,1)}, u32[]{:S(2)}) copy-start(pred[2,256,1024]{2,1,0:T(8,128)(4,1)} %broadcast_compare_fusion) | copy-start | bytes 1572868
  102.5 15.3 %copy-start.30 = (f32[2,16,256]{2,0,1:T(2,128)}, f32[2,16,256]{2,0,1:T(2,128)S(1)}, u32[]{:S(2)}) copy-start(f32[2,16,256]{2,0,1:T(2,128)S(1)} %copy.124) | copy-start | bytes 98308
  102.5 14.7 %copy-start.6 = (f32[16,256,2,64]{1,3,2,0:T(8,128)S(1)}, f32[16,256,2,64]{1,3,2,0:T(8,128)}, u32[]{:S(2)}) copy-start(f32[16,256,2,64]{1,3,2,0:T(8,128)} %get-tuple-element.37) | copy-start | bytes 6291460
  118.4 6.6 copy-start.11
  118.4 6.6 copy-start.29
  125.5 15.7 %copy-start.22 = (bf16[1024,1024]{1,0:T(8,128)(2,1)S(1)}, bf16[1024,1024]{1,0:T(8,128)(2,1)}, u32[]{:S(2)}) copy-start(bf16[1024,1024]{1,0:T(8,128)(2,1)} %param.24) | copy-start | bytes 6291460
  125.5 15.7 %copy-start.28 = (bf16[256,2,1024]{2,1,0:T(2,128)(2,1)S(1)}, bf16[256,2,1024]{2,1,0:T(2,128)(2,1)}, u32[]{:S(2)}) copy-start(bf16[256,2,1024]{2,1,0:T(2,128)(2,1)} %param.16) | copy-start | bytes 3145732
  141.2 2.7 copy-start.41
  141.2 2.7 copy-start.47
  142.6 1.3 copy-start.2
  142.6 278.5 %copy-start.37 = (f32[256,2]{0,1:T(2,128)}, f32[256,2]{0,1:T(2,128)S(1)}, u32[]{:S(2)}) copy-start(f32[256,2]{0,1:T(2,128)S(1)} %broadcast_multiply_fusion.5) | copy-start | bytes 6148
  143.9 277.2 %copy-start.39 = (f32[256,2]{0,1:T(2,128)}, f32[256,2]{0,1:T(2,128)S(1)}, u32[]{:S(2)}) copy-start(f32[256,2]{0,1:T(2,128)S(1)} %add_rsqrt_fusion.1) | copy-start | bytes 6148
  145.3 143.3 %reduce-scatter.5.cloned.1.call-start = ((), (), s32[]{:S(2)}) async-start(), calls=%async_computation.6 | async-start | bytes 10485760 | tf_op jit(solution)/shard_map/reduce_scatter | solution.py:136
  180.0 12.6 %copy-start.52 = (bf16[1024,1024]{1,0:T(8,128)(2,1)S(1)}, bf16[1024,1024]{1,0:T(8,128)(2,1)}, u32[]{:S(2)}) copy-start(bf16[1024,1024]{1,0:T(8,128)(2,1)} %param.28) | copy-start | bytes 6291460
  189.3 3.3 copy-start.56
  216.7 75.3 %copy-start.42 = (f32[1024]{0:T(1024)S(1)}, f32[1024]{0:T(1024)}, u32[]{:S(2)}) copy-start(f32[1024]{0:T(1024)} %param.29) | copy-start | bytes 12292
  216.8 113.0 %all-gather.8.cloned.1.call-start = ((), (), s32[]{:S(2)}) async-start(), calls=%async_computation.7 | async-start | bytes 5242880 | tf_op jit(solution)/shard_map/all_gather | solution.py:149
  288.7 3.4 copy-start.10
  291.6 1.6 copy-start.5
  295.1 121.2 %reduce-scatter.7.cloned.1.call-start = ((), (), s32[]{:S(2)}) async-start(), calls=%async_computation.8 | async-start | bytes 10485760 | tf_op jit(solution)/shard_map/reduce_scatter | solution.py:156
  344.4 71.9 %copy-start.3 = (f32[256,2,1024]{2,0,1:T(8,128)S(1)}, f32[256,2,1024]{2,0,1:T(8,128)}, u32[]{:S(2)}) copy-start(f32[256,2,1024]{2,0,1:T(8,128)} %copy-done.2) | copy-start | bytes 6291460
  344.4 71.9 %copy-start.51 = (f32[1024]{0:T(1024)S(1)}, f32[1024]{0:T(1024)}, u32[]{:S(2)}) copy-start(f32[1024]{0:T(1024)} %param.30) | copy-start | bytes 12292
  344.4 209.6 %reduce-scatter.9.cloned.1.call-start = ((), (), s32[]{:S(2)}) async-start(), calls=%async_computation.9 | async-start | bytes 5242880 | tf_op jit(solution)/shard_map/reduce_scatter | solution.py:204
  416.3 6.2 copy-start.23
  421.1 1.3 copy-start.16
  421.1 3.9 copy-start.43
  421.1 3.8 copy-start.45
  422.5 4.8 copy-start.15
  427.2 26.8 %copy-start.7 = (f32[16,256,2,64]{1,3,2,0:T(8,128)S(1)}, f32[16,256,2,64]{1,3,2,0:T(8,128)}, u32[]{:S(2)}) copy-start(f32[16,256,2,64]{1,3,2,0:T(8,128)} %get-tuple-element.37) | copy-start | bytes 6291460
  427.2 26.8 %copy-start.19 = (bf16[256,2,1024]{0,2,1:T(8,128)(2,1)S(1)}, bf16[256,2,1024]{0,2,1:T(8,128)(2,1)}, u32[]{:S(2)}) copy-start(bf16[256,2,1024]{0,2,1:T(8,128)(2,1)} %copy.131) | copy-start | bytes 3145732
  427.3 26.8 %copy-start.26 = (bf16[64,16,64]{2,1,0:T(8,128)(2,1)S(1)}, bf16[64,16,64]{2,1,0:T(8,128)(2,1)}, u32[]{:S(2)}) copy-start(bf16[64,16,64]{2,1,0:T(8,128)(2,1)} %reshape.110) | copy-start | bytes 393220
  427.3 26.8 %copy-start.31 = (f32[2,16,256]{2,0,1:T(2,128)S(1)}, f32[2,16,256]{2,0,1:T(2,128)}, u32[]{:S(2)}) copy-start(f32[2,16,256]{2,0,1:T(2,128)} %copy-done.30) | copy-start | bytes 98308
  427.3 26.8 %copy-start.33 = (f32[2,16,256]{2,0,1:T(2,128)S(1)}, f32[2,16,256]{2,0,1:T(2,128)}, u32[]{:S(2)}) copy-start(f32[2,16,256]{2,0,1:T(2,128)} %copy-done.32) | copy-start | bytes 98308
  427.3 26.8 %copy-start.50 = (pred[2,64]{1,0:T(4,128)(4,1)S(1)}, pred[2,64]{1,0:T(4,128)(4,1)}, u32[]{:S(2)}) copy-start(pred[2,64]{1,0:T(4,128)(4,1)} %copy-done.49) | copy-start | bytes 388
  456.1 28.1 %copy-start.34 = (f32[2,16,256]{2,1,0:T(8,128)}, f32[2,16,256]{2,1,0:T(8,128)S(1)}, u32[]{:S(2)}) copy-start(f32[2,16,256]{2,1,0:T(8,128)S(1)} %copy_add_fusion) | copy-start | bytes 98308
  456.1 28.1 %copy-start.9 = (bf16[256,2,1024]{0,2,1:T(8,128)(2,1)S(1)}, bf16[256,2,1024]{0,2,1:T(8,128)(2,1)}, u32[]{:S(2)}) copy-start(bf16[256,2,1024]{0,2,1:T(8,128)(2,1)} %copy-done.8) | copy-start | bytes 3145732
  501.2 91.9 %reduce-scatter.11.cloned.1.call-start = ((), (), s32[]{:S(2)}) async-start(), calls=%async_computation.10 | async-start | bytes 5242880 | tf_op jit(solution)/shard_map/reduce_scatter | solution.py:210
  527.0 0.9 copy-start.21
  527.0 1.9 copy-start.35
  527.0 200.3 %all-reduce.3.cloned.1.call-start = ((), (), s32[]{:S(2)}) async-start(), calls=%async_computation.11 | async-start | bytes 1048576 | tf_op jit(solution)/shard_map/psum | solution.py:223
  531.3 1.0 copy-start.12
  531.3 4.7 copy-start.18
  538.1 13.8 %copy-start.13 = (bf16[2,16,256,64]{2,3,0,1:T(8,128)(2,1)S(1)}, bf16[2,16,256,64]{2,3,0,1:T(8,128)(2,1)}, u32[]{:S(2)}) copy-start(bf16[2,16,256,64]{2,3,0,1:T(8,128)(2,1)} %copy-done.12) | copy-start | bytes 3145732
  538.1 13.8 %copy-start.25 = (bf16[64,16,64]{0,2,1:T(8,128)(2,1)S(1)}, bf16[64,16,64]{0,2,1:T(8,128)(2,1)}, u32[]{:S(2)}) copy-start(bf16[64,16,64]{0,2,1:T(8,128)(2,1)} %copy.137) | copy-start | bytes 393220
  553.9 39.2 %copy-start.54 = (bf16[1024,1024]{1,0:T(8,128)(2,1)S(1)}, bf16[1024,1024]{1,0:T(8,128)(2,1)}, u32[]{:S(2)}) copy-start(bf16[1024,1024]{1,0:T(8,128)(2,1)} %param.23) | copy-start | bytes 6291460
  558.7 37.1 %copy-start.38 = (f32[256,2]{0,1:T(2,128)S(1)}, f32[256,2]{0,1:T(2,128)}, u32[]{:S(2)}) copy-start(f32[256,2]{0,1:T(2,128)} %copy-done.37) | copy-start | bytes 6148
  558.7 37.1 %copy-start.40 = (f32[256,2]{0,1:T(2,128)S(1)}, f32[256,2]{0,1:T(2,128)}, u32[]{:S(2)}) copy-start(f32[256,2]{0,1:T(2,128)} %copy-done.39) | copy-start | bytes 6148
  558.7 37.1 %copy-start.44 = (f32[256,2]{0,1:T(2,128)S(1)}, f32[256,2]{0,1:T(2,128)}, u32[]{:S(2)}) copy-start(f32[256,2]{0,1:T(2,128)} %copy-done.43) | copy-start | bytes 6148
  558.7 37.1 %copy-start.46 = (f32[256,2]{0,1:T(2,128)S(1)}, f32[256,2]{0,1:T(2,128)}, u32[]{:S(2)}) copy-start(f32[256,2]{0,1:T(2,128)} %copy-done.45) | copy-start | bytes 6148
  593.1 2.7 copy-start.4
  593.1 2.7 copy-start.17
  593.1 3.2 copy-start.24
  596.3 134.4 %copy-start.1 = (bf16[1024,1024]{1,0:T(8,128)(2,1)S(1)}, bf16[1024,1024]{1,0:T(8,128)(2,1)}, u32[]{:S(2)}) copy-start(bf16[1024,1024]{1,0:T(8,128)(2,1)} %param.27) | copy-start | bytes 6291460
  (1 other events, 0.6 us)
Sparse Core Ops, SparseCore 0:
  13.5 60.9 all-gather.3
  145.4 34.4 all-gather.5
  216.9 71.7 reduce-scatter.4
  295.2 34.4 all-gather.7
  344.5 71.7 reduce-scatter.6
  501.3 44.5 reduce-scatter.8
  548.6 44.5 reduce-scatter.10
  599.2 128.1 all-reduce.2
where the time goes:
time: 742 us; the launch traced here: 738 us
  waiting for transfers between devices  419 us (56%)
  matrix products  182 us (25%)
  other arithmetic  61.8 us (8%)
  local copies, waits for them, and re-layouts  58 us (8%)
  between operations  15 us (2%)
    psum x1, waiting for transfers between devices, on_device(): lax.psum((prefix_kpart, prefix_vpart), ('rows', 'wide'))  124 us
    reduce_scatter x1, waiting for transfers between devices, on_device(): lax.psum_scatter(jnp.einsum('lrf,fd->lrd', hidden_act, w_down, preferred_...  71.8 us
    reduce_scatter x1, waiting for transfers between devices, on_device(): lax.psum_scatter(jnp.einsum('lrf,df->lrd', pre_rows, w_up, preferred_elem...  71.4 us
    all_gather x1, waiting for transfers between devices, on_device(): pair_all = lax.all_gather(pair_own, 'wide', axis=0, tiled=True)  48.4 us
    all_gather x1, waiting for transfers between devices, on_device(): lax.all_gather(grad_ffn, 'wide', axis=0, tiled=True)  34.6 us
    reduce_scatter x1, waiting for transfers between devices, on_device(): lax.psum_scatter(value_part.reshape(seq_total, row_count, model_width).as...  34.4 us
    all_gather x1, waiting for transfers between devices, on_device(): hidden_pre = up_rows(lax.all_gather(normed_low, 'wide', axis=0, tiled=True))  34.4 us
    convert_element_type x1, other arithmetic, on_device(): seq_ds = (seq_prob * (seq_grad - grad_delta)).astype(jnp.bfloat16)  28 us
  transfers between devices with their start and end apart: 8, of which 7 were waited for; matrix products, arithmetic and copies ran while one was open for 11% of the time, Pallas kernels for 0%

commit v1 on v0

--- a/solution.py
+++ b/solution.py
@@ -220,7 +220,9 @@
         + project_back(key_grad.astype(jnp.bfloat16), w_key)
         + project_back(value_grad.astype(jnp.bfloat16), w_value)
     )
-    prefix_key_grad, prefix_value_grad = lax.psum((prefix_kpart, prefix_vpart), ("rows", "wide"))
+    prefix_key_grad, prefix_value_grad = lax.psum(
+        lax.psum((prefix_kpart, prefix_vpart), "wide"), "rows"
+    )
     return (block_out, input_grad, prefix_key_grad, prefix_value_grad)
 
 

time: 742 us -> 707 us (0.953)
  waiting for transfers between devices: 419 us -> 389 us
    psum x1 -> x2, waiting for transfers between devices: 124 us -> 66.2 us  [the longest x1 66.1 us: on_device(): lax.psum(lax.psum((prefix_kpart, prefix_vpart), 'wide'), 'rows')]
    reduce_scatter x1, waiting for transfers between devices: 0.02 us -> 19.8 us  [on_device(): lax.psum_scatter(key_part.reshape(seq_total, row_count, model_width).asty...]
    reduce_scatter x1, waiting for transfers between devices: 34.4 us -> 42.7 us  [on_device(): lax.psum_scatter(value_part.reshape(seq_total, row_count, model_width).as...]
  transfers between devices with their start and end apart: 8 -> 9, of which waited for: 7 -> 8; matrix products, arithmetic and copies ran while one was open for 11% -> 12% of each run, Pallas kernels for 0% -> 0%
where the time goes in v1:
time: 707 us; the launch traced here: 703 us
  waiting for transfers between devices  389 us (55%)
  matrix products  177 us (25%)
  local copies, waits for them, and re-layouts  60.2 us (9%)
  other arithmetic  59.9 us (8%)
  between operations  14.7 us (2%)
    reduce_scatter x1, waiting for transfers between devices, on_device(): lax.psum_scatter(jnp.einsum('lrf,fd->lrd', hidden_act, w_down, preferred_...  71.8 us
    reduce_scatter x1, waiting for transfers between devices, on_device(): lax.psum_scatter(jnp.einsum('lrf,df->lrd', pre_rows, w_up, preferred_elem...  71.6 us
    psum x1, waiting for transfers between devices, on_device(): lax.psum(lax.psum((prefix_kpart, prefix_vpart), 'wide'), 'rows')  66.1 us
    all_gather x1, waiting for transfers between devices, on_device(): pair_all = lax.all_gather(pair_own, 'wide', axis=0, tiled=True)  48.4 us
    reduce_scatter x1, waiting for transfers between devices, on_device(): lax.psum_scatter(value_part.reshape(seq_total, row_count, model_width).as...  42.7 us
    all_gather x1, waiting for transfers between devices, on_device(): lax.all_gather(grad_ffn, 'wide', axis=0, tiled=True)  34.6 us
    all_gather x1, waiting for transfers between devices, on_device(): hidden_pre = up_rows(lax.all_gather(normed_low, 'wide', axis=0, tiled=True))  34.2 us
    convert_element_type x1, other arithmetic, on_device(): seq_ds = (seq_prob * (seq_grad - grad_delta)).astype(jnp.bfloat16)  27.8 us
  transfers between devices with their start and end apart: 9, of which 8 were waited for; matrix products, arithmetic and copies ran while one was open for 12% of the time, Pallas kernels for 0%

profile of v1, /device:TPU:0, one launch (start us, length us, event | category | flops | bytes accessed | tf_op | source)
XLA Modules:
  0.0 702.9 jit_solution(12681732265456038789)
XLA Ops:
  7.3 3.3 fusion.75
  10.6 1.3 fusion.78
  11.9 1.5 pad_maximum_fusion
  13.5 3.9 multiply_convert_fusion.1
  17.4 1.6 copy.119
  19.2 2.0 reshape.110
  21.2 1.9 copy.128
  23.2 1.2 broadcast_compare_fusion
  24.3 1.8 bitcast_reduce_fusion
  26.1 48.4 %all-gather.4.cloned.1.call-done = bf16[1024,2,2048]{2,0,1:T(8,128)(2,1)} async-done(((bf16[256,2,2048]{2,0,1:T(8,128)(2,1)}), bf16[1024,2,2048]{2,0,1:T(8,128)(2,1)}) %all-gather.4.cloned.1.call-update) | async-done | bytes 8388624 | tf_op jit(solution)/shard_map/all_gather | solution.py:109
  74.5 6.0 fusion.148
  80.5 6.2 copy.120
  86.7 15.8 %select_reduce_fusion = (f32[2,16,256]{2,1,0:T(8,128)S(1)}, f32[2,16,256,1024]{3,2,1,0:T(8,128)}) fusion(pred[2,256,1024]{2,1,0:T(8,128)(4,1)} %broadcast_compare_fusion, bf16[256,2,16,64]{0,3,2,1:T(8,128)(2,1)S(1)} %bitcast.137, bf16[1024,2,16,64]{0,3,2,1:T(8,128)(2,1)} %bitcast.134), kind=kOutput, calls=%fused_computation.3 | convolution fusion | flops 1090510848 | bytes 39354368 | tf_op jit(solution)/shard_map/crhe,lrhe->rhcl/dot_general | solution.py:54
  102.6 14.7 %fusion.1 = f32[2,16,256]{2,1,0:T(8,128)S(1)} fusion(f32[2,16,256,1024]{3,2,1,0:T(8,128)} %get-tuple-element.37, f32[2,16,256]{2,1,0:T(8,128)S(1)} %copy_maximum_fusion, pred[2,256,1024]{2,1,0:T(8,128)(4,1)S(1)} %copy-done.15), kind=kLoop, calls=%fused_computation.5 | loop fusion | flops 25157632 | bytes 34144256 | tf_op jit(solution)/shard_map/reduce_sum | solution.py:67
  117.3 0.5 fusion.65
  117.9 0.5 fusion.142
  118.5 6.6 copy.117
  125.5 15.7 %fusion.42 = bf16[256,2,16,64]{0,3,2,1:T(8,128)(2,1)S(1)} fusion(f32[16,2,256,64]{2,3,0,1:T(8,128)S(1)} %fusion.96, bf16[1024,2,16,64]{0,3,2,1:T(8,128)(2,1)} %bitcast.141, f32[2,16,256,1024]{3,2,1,0:T(8,128)} %get-tuple-element.37, f32[2,16,256]{2,1,0:T(8,128)S(1)} %copy_add_fusion.1, f32[2,16,256]{2,1,0:T(8,128)S(1)} %copy_maximum_fusion, ...), kind=kOutput, calls=%fused_computation.62 | convolution fusion | flops 1108344832 | bytes 41484288 | tf_op jit(solution)/shard_map/rhcl,lrhe->crhe/dot_general | solution.py:115
  141.2 1.4 fusion.149
  143.0 0.9 copy-done.2
  144.0 1.4 fusion.59
  145.4 0.4 reduce-scatter.5.cloned.1.call-start
  145.8 34.2 %all-gather.6.cloned.1.call-done = bf16[1024,2,1024]{2,0,1:T(8,128)(2,1)} async-done(((bf16[256,2,1024]{2,0,1:T(8,128)(2,1)}), bf16[1024,2,1024]{2,0,1:T(8,128)(2,1)}) %all-gather.6.cloned.1.call-update) | async-done | bytes 4194320 | tf_op jit(solution)/shard_map/all_gather | solution.py:134
  180.0 9.4 %fusion.57 = (u8[1024,1024]{1,0:T(8,128)(4,1)S(1)}, u8[1024,1024]{1,0:T(8,128)(4,1)S(1)}, f32[1024,2,1024]{2,0,1:T(8,128)S(1)}) fusion(bf16[1024,2,1024]{2,0,1:T(8,128)(2,1)} %all-gather.6.cloned.1.call-done, bf16[1024,1024]{1,0:T(8,128)(2,1)S(1)} %copy-done), kind=kOutput, calls=%fused_computation.92 | convolution fusion | flops 4320133120 | bytes 16777216 | tf_op jit(solution)/shard_map/lrd,df->lrf/dot_general | solution.py:132
  189.4 3.2 copy-done.56
  192.6 24.2 %fusion.21 = f32[1024,2,1024]{2,0,1:T(8,128)} fusion(f32[1024,2,1024]{2,0,1:T(8,128)S(1)} %get-tuple-element.42, bf16[1024,1024]{1,0:T(8,128)(2,1)S(1)} %copy-done.52, u8[1024,1024]{1,0:T(8,128)(4,1)S(1)} %get-tuple-element.21, u8[1024,1024]{1,0:T(8,128)(4,1)S(1)} %get-tuple-element.20), kind=kOutput, calls=%fused_computation.39 | convolution fusion | flops 4441767936 | bytes 20971520 | tf_op jit(solution)/shard_map/lrf,fd->lrd/dot_general | solution.py:137
  216.9 71.8 %reduce-scatter.5.cloned.1.call-done = f32[256,2,1024]{2,0,1:T(8,128)} async-done(((f32[1024,2,1024]{2,0,1:T(8,128)}), f32[256,2,1024]{2,0,1:T(8,128)}) %reduce-scatter.5.cloned.1.call-update) | async-done | bytes 2097168 | tf_op jit(solution)/shard_map/reduce_scatter | solution.py:136
  288.7 3.0 fusion.146
  292.1 1.2 fusion.72
  293.3 1.8 fusion.105
  295.2 34.6 %all-gather.8.cloned.1.call-done = bf16[1024,2,1024]{2,0,1:T(8,128)(2,1)} async-done(((bf16[256,2,1024]{2,0,1:T(8,128)(2,1)}), bf16[1024,2,1024]{2,0,1:T(8,128)(2,1)}) %all-gather.8.cloned.1.call-update) | async-done | bytes 4194320 | tf_op jit(solution)/shard_map/all_gather | solution.py:149
  329.8 14.7 %fusion.23 = f32[1024,2,1024]{2,0,1:T(8,128)} fusion(f32[1024,2,1024]{2,0,1:T(8,128)} %copy-done.56, bf16[1024,1024]{1,0:T(8,128)(2,1)S(1)} %copy-done, bf16[1024,2,1024]{2,0,1:T(8,128)(2,1)} %all-gather.8.cloned.1.call-done, bf16[1024,1024]{1,0:T(8,128)(2,1)} %param.28), kind=kOutput, calls=%fused_computation.40 | convolution fusion | flops 8610906112 | bytes 25165824 | tf_op jit(solution)/shard_map/lrf,df->lrd/dot_general | solution.py:157
  344.7 71.6 %reduce-scatter.7.cloned.1.call-done = f32[256,2,1024]{2,0,1:T(8,128)} async-done(((f32[1024,2,1024]{2,0,1:T(8,128)}), f32[256,2,1024]{2,0,1:T(8,128)}) %reduce-scatter.7.cloned.1.call-update) | async-done | bytes 2097168 | tf_op jit(solution)/shard_map/reduce_scatter | solution.py:156
  416.4 4.8 fusion.145
  421.2 1.3 copy-done.18
  422.5 2.5 fusion.81
  425.1 2.3 copy.131
  427.4 26.7 %multiply_reduce_fusion = (f32[2,16,256]{2,1,0:T(8,128)S(1)}, f32[2,16,256,1024]{3,2,1,0:T(8,128)}) fusion(f32[2,16,256]{2,1,0:T(8,128)S(1)} %copy_add_fusion.1, f32[2,16,256]{2,1,0:T(8,128)S(1)} %copy_maximum_fusion, f32[2,16,256,1024]{3,2,1,0:T(8,128)} %get-tuple-element.37, pred[2,256,1024]{2,1,0:T(8,128)(4,1)S(1)} %copy-done.16, ...), kind=kOutput, calls=%fused_computation.1 | convolution fusion | flops 1115676672 | bytes 72974336 | tf_op jit(solution)/shard_map/crhe,lrhe->rhcl/dot_general | solution.py:174
  454.2 1.2 fusion.94
  455.4 0.8 fusion.29
  456.2 0.8 fusion.31
  457.0 1.0 copy-done.13
  458.4 0.9 copy.142
  459.3 1.9 copy.144
  461.3 27.8 %multiply_convert_fusion = bf16[2,16,256,1024]{3,2,1,0:T(8,128)(2,1)} fusion(f32[2,16,256,1024]{3,2,1,0:T(8,128)} %get-tuple-element.44, f32[2,16,256]{2,1,0:T(8,128)S(1)} %copy_add_fusion, f32[2,16,256]{2,1,0:T(8,128)S(1)} %copy_add_fusion.1, f32[2,16,256]{2,1,0:T(8,128)S(1)} %copy_maximum_fusion, f32[2,16,256,1024]{3,2,1,0:T(8,128)} %get-tuple-element.37, ...), kind=kLoop, calls=%fused_computation | loop fusion | flops 50331648 | bytes 84508672 | tf_op jit(solution)/shard_map/convert_element_type | solution.py:183
  489.1 10.9 %convolution_convert_fusion = bf16[2,16,64,1024]{3,2,1,0:T(8,128)(2,1)} fusion(bf16[256,2,16,64]{0,3,2,1:T(8,128)(2,1)S(1)} %bitcast.139, bf16[2,16,256,1024]{3,2,1,0:T(8,128)(2,1)} %multiply_convert_fusion), kind=kOutput, calls=%fused_computation.41 | convolution fusion | flops 1075838976 | bytes 22020096 | tf_op jit(solution)/shard_map/rhcl,crhe->lrhe/dot_general | solution.py:196
  500.0 6.3 copy.139
  506.5 0.9 copy-done.22
  507.4 15.8 %fusion.25 = bf16[2,16,64,1024]{3,2,1,0:T(8,128)(2,1)} fusion(bf16[256,2,16,64]{0,3,2,1:T(8,128)(2,1)S(1)} %bitcast.147, f32[2,16,256,1024]{3,2,1,0:T(8,128)} %get-tuple-element.37, f32[2,16,256]{2,1,0:T(8,128)S(1)} %copy_add_fusion.1, f32[2,16,256]{2,1,0:T(8,128)S(1)} %copy_maximum_fusion, pred[2,256,1024]{2,1,0:T(8,128)(4,1)S(1)} %copy-done.17), kind=kOutput, calls=%fused_computation.42 | convolution fusion | flops 1109393408 | bytes 39387136 | tf_op jit(solution)/shard_map/rhcl,crhe->lrhe/dot_general | solution.py:199
  523.2 6.2 copy.140
  529.5 0.9 copy-done.24
  531.1 2.0 copy.145
  533.2 14.4 %fusion.150 = f32[2,16,64,256]{3,2,1,0:T(8,128)} fusion(bf16[1024,2,16,64]{0,3,2,1:T(8,128)(2,1)} %bitcast.135, bf16[2,16,256,1024]{3,2,1,0:T(8,128)(2,1)} %multiply_convert_fusion), kind=kOutput, calls=%fused_computation.180 | convolution fusion | flops 1073741824 | bytes 23068672 | tf_op jit(solution)/shard_map/rhcl,lrhe->crhe/dot_general | solution.py:185
  547.6 2.0 fusion.28
  549.6 19.8 %reduce-scatter.9.cloned.1.call-done = bf16[256,2,1024]{2,0,1:T(8,128)(2,1)} async-done(((bf16[1024,2,1024]{2,0,1:T(8,128)(2,1)}), bf16[256,2,1024]{2,0,1:T(8,128)(2,1)}) %reduce-scatter.9.cloned.1.call-update) | async-done | bytes 1048592 | tf_op jit(solution)/shard_map/reduce_scatter | solution.py:204
  569.5 4.6 fusion.52
  574.0 42.7 %reduce-scatter.11.cloned.1.call-done = bf16[256,2,1024]{2,0,1:T(8,128)(2,1)} async-done(((bf16[1024,2,1024]{2,0,1:T(8,128)(2,1)}), bf16[256,2,1024]{2,0,1:T(8,128)(2,1)}) %reduce-scatter.11.cloned.1.call-update) | async-done | bytes 1048592 | tf_op jit(solution)/shard_map/reduce_scatter | solution.py:210
  616.7 2.7 fusion.48
  619.4 0.4 copy-done.27
  619.9 3.9 add_add_fusion
  623.8 2.9 copy.146
  626.7 66.1 %all-reduce.5.cloned.1.call-done = (f32[64,1024]{1,0:T(8,128)}, f32[64,1024]{1,0:T(8,128)}) async-done(((f32[64,1024]{1,0:T(8,128)}, f32[64,1024]{1,0:T(8,128)}), (f32[64,1024]{1,0:T(8,128)}, f32[64,1024]{1,0:T(8,128)})) %all-reduce.5.cloned.1.call-update) | async-done | bytes 524304 | tf_op jit(solution)/shard_map/psum | solution.py:223
  692.8 1.7 copy.205
  694.5 1.7 copy.206
  (146 shorter events, 3.7 us)
Async XLA Ops:
  7.2 172.8 %copy-start = (bf16[1024,1024]{1,0:T(8,128)(2,1)S(1)}, bf16[1024,1024]{1,0:T(8,128)(2,1)}, u32[]{:S(2)}) copy-start(bf16[1024,1024]{1,0:T(8,128)(2,1)} %param.27) | copy-start | bytes 6291460
  7.2 3.4 copy-start.29
  7.2 67.3 %all-gather.4.cloned.1.call-start = ((), (), s32[]{:S(2)}) async-start(), calls=%async_computation.4 | async-start | bytes 10485760 | tf_op jit(solution)/shard_map/all_gather | solution.py:109
  7.2 3.3 copy-start.53
  13.4 166.6 %all-gather.6.cloned.1.call-start = ((), (), s32[]{:S(2)}) async-start(), calls=%async_computation.5 | async-start | bytes 5242880 | tf_op jit(solution)/shard_map/all_gather | solution.py:134
  13.5 5.6 copy-start.36
  13.5 9.7 %copy-start.48 = (s32[2,1024]{1,0:T(2,128)S(1)}, s32[2,1024]{1,0:T(2,128)}, u32[]{:S(2)}) copy-start(s32[2,1024]{1,0:T(2,128)} %param.17) | copy-start | bytes 24580
  13.5 9.7 %copy-start.55 = (s32[2,64]{1,0:T(2,128)S(1)}, s32[2,64]{1,0:T(2,128)}, u32[]{:S(2)}) copy-start(s32[2,64]{1,0:T(2,128)} %param.18) | copy-start | bytes 1540
  19.0 67.7 %copy-start.8 = (bf16[256,2,1024]{0,2,1:T(8,128)(2,1)}, bf16[256,2,1024]{0,2,1:T(8,128)(2,1)S(1)}, u32[]{:S(2)}) copy-start(bf16[256,2,1024]{0,2,1:T(8,128)(2,1)S(1)} %copy.119) | copy-start | bytes 3145732
  19.2 61.3 %copy-start.23 = (bf16[64,16,64]{2,1,0:T(8,128)(2,1)}, bf16[64,16,64]{2,1,0:T(8,128)(2,1)S(1)}, u32[]{:S(2)}) copy-start(bf16[64,16,64]{2,1,0:T(8,128)(2,1)S(1)} %reshape.109) | copy-start | bytes 393220
  23.1 94.7 %copy-start.49 = (pred[2,64]{1,0:T(4,128)(4,1)}, pred[2,64]{1,0:T(4,128)(4,1)S(1)}, u32[]{:S(2)}) copy-start(pred[2,64]{1,0:T(4,128)(4,1)S(1)} %broadcast_compare_fusion.1) | copy-start | bytes 388
  86.7 15.9 %copy-start.15 = (pred[2,256,1024]{2,1,0:T(8,128)(4,1)S(1)}, pred[2,256,1024]{2,1,0:T(8,128)(4,1)}, u32[]{:S(2)}) copy-start(pred[2,256,1024]{2,1,0:T(8,128)(4,1)} %broadcast_compare_fusion) | copy-start | bytes 1572868
  102.6 15.3 %copy-start.32 = (f32[2,16,256]{2,0,1:T(2,128)}, f32[2,16,256]{2,0,1:T(2,128)S(1)}, u32[]{:S(2)}) copy-start(f32[2,16,256]{2,0,1:T(2,128)S(1)} %copy.124) | copy-start | bytes 98308
  102.6 14.7 %copy-start.6 = (f32[16,256,2,64]{1,3,2,0:T(8,128)S(1)}, f32[16,256,2,64]{1,3,2,0:T(8,128)}, u32[]{:S(2)}) copy-start(f32[16,256,2,64]{1,3,2,0:T(8,128)} %get-tuple-element.39) | copy-start | bytes 6291460
  118.5 6.6 copy-start.11
  118.5 6.6 copy-start.31
  125.5 15.7 %copy-start.25 = (bf16[1024,1024]{1,0:T(8,128)(2,1)S(1)}, bf16[1024,1024]{1,0:T(8,128)(2,1)}, u32[]{:S(2)}) copy-start(bf16[1024,1024]{1,0:T(8,128)(2,1)} %param.24) | copy-start | bytes 6291460
  125.5 15.7 %copy-start.30 = (bf16[256,2,1024]{2,1,0:T(2,128)(2,1)S(1)}, bf16[256,2,1024]{2,1,0:T(2,128)(2,1)}, u32[]{:S(2)}) copy-start(bf16[256,2,1024]{2,1,0:T(2,128)(2,1)} %param.16) | copy-start | bytes 3145732
  141.2 2.7 copy-start.41
  141.2 2.7 copy-start.47
  142.6 1.3 copy-start.2
  142.7 278.6 %copy-start.37 = (f32[256,2]{0,1:T(2,128)}, f32[256,2]{0,1:T(2,128)S(1)}, u32[]{:S(2)}) copy-start(f32[256,2]{0,1:T(2,128)S(1)} %broadcast_multiply_fusion.5) | copy-start | bytes 6148
  144.0 277.3 %copy-start.39 = (f32[256,2]{0,1:T(2,128)}, f32[256,2]{0,1:T(2,128)S(1)}, u32[]{:S(2)}) copy-start(f32[256,2]{0,1:T(2,128)S(1)} %add_rsqrt_fusion.1) | copy-start | bytes 6148
  145.4 143.4 %reduce-scatter.5.cloned.1.call-start = ((), (), s32[]{:S(2)}) async-start(), calls=%async_computation.6 | async-start | bytes 10485760 | tf_op jit(solution)/shard_map/reduce_scatter | solution.py:136
  180.0 12.6 %copy-start.52 = (bf16[1024,1024]{1,0:T(8,128)(2,1)S(1)}, bf16[1024,1024]{1,0:T(8,128)(2,1)}, u32[]{:S(2)}) copy-start(bf16[1024,1024]{1,0:T(8,128)(2,1)} %param.28) | copy-start | bytes 6291460
  189.4 3.3 copy-start.56
  216.8 75.2 %copy-start.42 = (f32[1024]{0:T(1024)S(1)}, f32[1024]{0:T(1024)}, u32[]{:S(2)}) copy-start(f32[1024]{0:T(1024)} %param.29) | copy-start | bytes 12292
  216.9 112.9 %all-gather.8.cloned.1.call-start = ((), (), s32[]{:S(2)}) async-start(), calls=%async_computation.7 | async-start | bytes 5242880 | tf_op jit(solution)/shard_map/all_gather | solution.py:149
  288.7 3.4 copy-start.10
  291.7 1.6 copy-start.5
  295.2 121.2 %reduce-scatter.7.cloned.1.call-start = ((), (), s32[]{:S(2)}) async-start(), calls=%async_computation.8 | async-start | bytes 10485760 | tf_op jit(solution)/shard_map/reduce_scatter | solution.py:156
  344.5 71.9 %copy-start.3 = (f32[256,2,1024]{2,0,1:T(8,128)S(1)}, f32[256,2,1024]{2,0,1:T(8,128)}, u32[]{:S(2)}) copy-start(f32[256,2,1024]{2,0,1:T(8,128)} %copy-done.2) | copy-start | bytes 6291460
  344.5 71.9 %copy-start.51 = (f32[1024]{0:T(1024)S(1)}, f32[1024]{0:T(1024)}, u32[]{:S(2)}) copy-start(f32[1024]{0:T(1024)} %param.30) | copy-start | bytes 12292
  344.5 205.1 %all-reduce.7.cloned.1.call-start = ((), (), s32[]{:S(2)}) async-start(), calls=%async_computation.12 | async-start | bytes 1048576 | tf_op jit(solution)/shard_map/psum | solution.py:224
  416.3 6.2 copy-start.26
  421.2 1.4 copy-start.18
  421.2 3.9 copy-start.43
  421.2 3.9 copy-start.45
  422.5 4.8 copy-start.16
  427.4 26.8 %copy-start.12 = (bf16[2,16,256,64]{2,3,0,1:T(8,128)(2,1)S(1)}, bf16[2,16,256,64]{2,3,0,1:T(8,128)(2,1)}, u32[]{:S(2)}) copy-start(bf16[2,16,256,64]{2,3,0,1:T(8,128)(2,1)} %copy-done.11) | copy-start | bytes 3145732
  427.4 26.8 %copy-start.21 = (bf16[256,2,1024]{0,2,1:T(8,128)(2,1)S(1)}, bf16[256,2,1024]{0,2,1:T(8,128)(2,1)}, u32[]{:S(2)}) copy-start(bf16[256,2,1024]{0,2,1:T(8,128)(2,1)} %copy.131) | copy-start | bytes 3145732
  427.4 28.0 %copy-start.7 = (f32[16,256,2,64]{1,3,2,0:T(8,128)S(1)}, f32[16,256,2,64]{1,3,2,0:T(8,128)}, u32[]{:S(2)}) copy-start(f32[16,256,2,64]{1,3,2,0:T(8,128)} %get-tuple-element.39) | copy-start | bytes 6291460
  427.4 28.0 %copy-start.28 = (bf16[64,16,64]{2,1,0:T(8,128)(2,1)S(1)}, bf16[64,16,64]{2,1,0:T(8,128)(2,1)}, u32[]{:S(2)}) copy-start(bf16[64,16,64]{2,1,0:T(8,128)(2,1)} %reshape.110) | copy-start | bytes 393220
  427.4 28.0 %copy-start.33 = (f32[2,16,256]{2,0,1:T(2,128)S(1)}, f32[2,16,256]{2,0,1:T(2,128)}, u32[]{:S(2)}) copy-start(f32[2,16,256]{2,0,1:T(2,128)} %copy-done.32) | copy-start | bytes 98308
  427.4 28.0 %copy-start.35 = (f32[2,16,256]{2,0,1:T(2,128)S(1)}, f32[2,16,256]{2,0,1:T(2,128)}, u32[]{:S(2)}) copy-start(f32[2,16,256]{2,0,1:T(2,128)} %copy-done.34) | copy-start | bytes 98308
  427.4 28.0 %copy-start.50 = (pred[2,64]{1,0:T(4,128)(4,1)S(1)}, pred[2,64]{1,0:T(4,128)(4,1)}, u32[]{:S(2)}) copy-start(pred[2,64]{1,0:T(4,128)(4,1)} %copy-done.49) | copy-start | bytes 388
  456.2 1.8 copy-start.9
  458.0 3.3 copy-start.17
  489.0 80.4 %reduce-scatter.9.cloned.1.call-start = ((), (), s32[]{:S(2)}) async-start(), calls=%async_computation.9 | async-start | bytes 5242880 | tf_op jit(solution)/shard_map/reduce_scatter | solution.py:204
  506.2 1.2 copy-start.22
  506.2 110.5 %reduce-scatter.11.cloned.1.call-start = ((), (), s32[]{:S(2)}) async-start(), calls=%async_computation.10 | async-start | bytes 5242880 | tf_op jit(solution)/shard_map/reduce_scatter | solution.py:210
  529.5 1.0 copy-start.24
  529.5 1.7 copy-start.20
  529.5 163.3 %all-reduce.5.cloned.1.call-start = ((), (), s32[]{:S(2)}) async-start(), calls=%async_computation.11 | async-start | bytes 1048576 | tf_op jit(solution)/shard_map/psum | solution.py:223
  533.2 14.4 %copy-start.14 = (bf16[2,16,256,64]{2,3,0,1:T(8,128)(2,1)S(1)}, bf16[2,16,256,64]{2,3,0,1:T(8,128)(2,1)}, u32[]{:S(2)}) copy-start(bf16[2,16,256,64]{2,3,0,1:T(8,128)(2,1)} %copy-done.13) | copy-start | bytes 3145732
  549.6 67.1 %copy-start.54 = (bf16[1024,1024]{1,0:T(8,128)(2,1)S(1)}, bf16[1024,1024]{1,0:T(8,128)(2,1)}, u32[]{:S(2)}) copy-start(bf16[1024,1024]{1,0:T(8,128)(2,1)} %param.23) | copy-start | bytes 6291460
  574.0 45.4 %copy-start.38 = (f32[256,2]{0,1:T(2,128)S(1)}, f32[256,2]{0,1:T(2,128)}, u32[]{:S(2)}) copy-start(f32[256,2]{0,1:T(2,128)} %copy-done.37) | copy-start | bytes 6148
  574.0 45.4 %copy-start.40 = (f32[256,2]{0,1:T(2,128)S(1)}, f32[256,2]{0,1:T(2,128)}, u32[]{:S(2)}) copy-start(f32[256,2]{0,1:T(2,128)} %copy-done.39) | copy-start | bytes 6148
  574.0 45.4 %copy-start.44 = (f32[256,2]{0,1:T(2,128)S(1)}, f32[256,2]{0,1:T(2,128)}, u32[]{:S(2)}) copy-start(f32[256,2]{0,1:T(2,128)} %copy-done.43) | copy-start | bytes 6148
  574.0 45.4 %copy-start.46 = (f32[256,2]{0,1:T(2,128)S(1)}, f32[256,2]{0,1:T(2,128)}, u32[]{:S(2)}) copy-start(f32[256,2]{0,1:T(2,128)} %copy-done.45) | copy-start | bytes 6148
  616.7 2.7 copy-start.4
  616.7 2.7 copy-start.19
  616.7 3.2 copy-start.27
  619.9 76.3 %copy-start.1 = (bf16[1024,1024]{1,0:T(8,128)(2,1)S(1)}, bf16[1024,1024]{1,0:T(8,128)(2,1)}, u32[]{:S(2)}) copy-start(bf16[1024,1024]{1,0:T(8,128)(2,1)} %param.27) | copy-start | bytes 6291460
  (2 other events, 1.6 us)
Sparse Core Ops, SparseCore 0:
  13.5 60.9 all-gather.3
  145.5 34.4 all-gather.5
  217.0 71.7 reduce-scatter.4
  295.3 34.4 all-gather.7
  344.6 71.6 reduce-scatter.6
  489.2 33.1 all-reduce.6
  524.9 44.5 reduce-scatter.8
  572.1 44.5 reduce-scatter.10
  620.2 72.6 all-reduce.4
